TPU v7x, 32 devices: a whole 2x2x4 slice. The times are simulated.
32 devices in a mesh: seq: 8 (over z, y), fsdp: 4 (over x, core).
Axes of the slice: x: 2, y: 2, z: 4, core: 2. Of those that a mesh axis runs over, the one named last changes fastest.
Arguments:
- hidden_in: bfloat16 [4, 1024, 2048], P('fsdp', 'seq'), may hold values from -18 to 18
- ln1_gain: bfloat16 [2048], P(('seq', 'fsdp')), may hold values from 0.5 to 1.5
- ln1_bias: bfloat16 [2048], P(('seq', 'fsdp')), may hold values from -1.1953125 to 1.1953125
- qkv_weight: bfloat16 [2048, 6144], P(('seq', 'fsdp')), may hold values from -0.125 to 0.125
- qkv_bias: bfloat16 [3, 2048], P(None, ('seq', 'fsdp')), may hold values from -3 to 3
- out_weight: bfloat16 [2048, 2048], P(('seq', 'fsdp')), may hold values from -3 to 3
- ln2_gain: bfloat16 [2048], P(('seq', 'fsdp')), may hold values from 0.5 to 1.5
- ln2_bias: bfloat16 [2048], P(('seq', 'fsdp')), may hold values from -1.1953125 to 1.1953125
- gate_weight: bfloat16 [2048, 5632], P(('seq', 'fsdp')), may hold values from -0.125 to 0.125
- up_weight: bfloat16 [2048, 5632], P(('seq', 'fsdp')), may hold values from -0.125 to 0.125
- down_weight: bfloat16 [5632, 2048], P(('seq', 'fsdp')), may hold values from -0.078125 to 0.078125
- seq_lengths: int32 [4, 3], P('fsdp'), may hold values from 1 to 512, 640 in all within a row
- deal_order: int32 [4, 1024], P('fsdp'), may hold values from 0 to 1023, each once within a row
- out_grad: bfloat16 [4, 1024, 2048], P('fsdp', 'seq'), may hold values from -6 to 6
Outputs:
- layer_out: bfloat16 [4, 1024, 2048], P('fsdp', 'seq')
- input_grad: float32 [4, 1024, 2048], P('fsdp', 'seq')
- ln1_gain_grad: float32 [2048], P(('seq', 'fsdp'))
- ln1_bias_grad: float32 [2048], P(('seq', 'fsdp'))
- qkv_weight_grad: float32 [2048, 6144], P(('seq', 'fsdp'))
- qkv_bias_grad: float32 [3, 2048], P(None, ('seq', 'fsdp'))
- out_weight_grad: float32 [2048, 2048], P(('seq', 'fsdp'))
- ln2_gain_grad: float32 [2048], P(('seq', 'fsdp'))
- ln2_bias_grad: float32 [2048], P(('seq', 'fsdp'))
- gate_weight_grad: float32 [2048, 5632], P(('seq', 'fsdp'))
- up_weight_grad: float32 [2048, 5632], P(('seq', 'fsdp'))
- down_weight_grad: float32 [5632, 2048], P(('seq', 'fsdp'))
- branch_rms: float32 [3], replicated
Inputs may be any that keep to these rules, and one draw needn't show every extreme that they name: `seq_lengths`: each group's lengths sum to 640, and its longest is exactly 512. `deal_order`: each group's row is a permutation of its positions.
All inputs are finite; a program needn't handle non-finite values.
Results may differ from a plain program's by a relative error of at most 0.00705.
The roundings to bfloat16 on the way count: a program that leaves them out, or rounds other values in their place, can miss the bound.
Values may be sent and summed in bfloat16 or wider, within the bound.
A program may use at most 384 MiB of HBM per device.

v0:
```python
import jax
import jax.numpy as jnp
from jax import lax
from jax.sharding import PartitionSpec as P

HEAD_DIM = 64
ROT = 16
EPS = 1e-05


def normalize(values):
    center = values - jnp.mean(values, -1, keepdims=True)
    spread = jnp.mean(center * center, -1, keepdims=True)
    rstd = lax.rsqrt(spread + EPS)
    return (center * rstd, rstd)


def norm_back(grad, normed, rstd, gain):
    scaled = grad * gain
    inner = (
        scaled
        - jnp.mean(scaled, -1, keepdims=True)
        - normed * jnp.mean(scaled * normed, -1, keepdims=True)
    )
    return (rstd * inner, jnp.sum(grad * normed, 0), jnp.sum(grad, 0))


def segment_of(pos, lengths):
    nseg = lengths.shape[0]
    ends = jnp.cumsum(lengths)
    seg = jnp.sum((pos[:, None] >= ends[None, :]).astype(jnp.int32), 1)
    starts = jnp.concatenate([jnp.zeros((1,), jnp.int32), ends[:-1]])
    start = jnp.sum(
        jnp.where(seg[:, None] == jnp.arange(nseg, dtype=jnp.int32)[None, :], starts[None, :], 0), 1
    )
    start = jnp.where(seg < nseg, start, pos)
    return (seg, start)


def rotate(values, rel, sign):
    count = values.shape[0]
    view = values.reshape(count, -1, HEAD_DIM)
    half = ROT // 2
    freq = 10000.0 ** (-2.0 * jnp.arange(half, dtype=jnp.float32) / ROT)
    angle = rel[:, None] * freq[None, :]
    cosine = jnp.cos(angle)[:, None, :]
    sine = jnp.sin(angle)[:, None, :]
    first = view[..., :half]
    second = view[..., half:ROT]
    turned = jnp.concatenate(
        [
            first * cosine - sign * second * sine,
            second * cosine + sign * first * sine,
            view[..., ROT:],
        ],
        -1,
    )
    return turned.reshape(count, -1)


def outer(left, right):
    return lax.dot_general(
        left, right, (((0,), (0,)), ((), ())), preferred_element_type=jnp.float32
    )


def times_transposed(left, right):
    return lax.dot_general(
        left, right, (((1,), (1,)), ((), ())), preferred_element_type=jnp.float32
    )


def mlp_forward(gate, upper):
    sigma = jax.nn.sigmoid(gate)
    return ((gate * sigma * upper).astype(jnp.bfloat16), sigma)


def mlp_backward(hidden_grad, gate, upper, sigma):
    up_act = (hidden_grad * gate * sigma).astype(jnp.bfloat16)
    gate_act = (hidden_grad * upper * sigma * (1.0 + gate * (1.0 - sigma))).astype(jnp.bfloat16)
    return (gate_act, up_act)


def body(
    hidden_in,
    ln1_gain,
    ln1_bias,
    qkv_weight,
    qkv_bias,
    out_weight,
    ln2_gain,
    ln2_bias,
    gate_weight,
    up_weight,
    down_weight,
    seq_lengths,
    deal_order,
    out_grad,
):
    rows = hidden_in.shape[1]
    width = hidden_in.shape[2]
    stream = hidden_in[0].astype(jnp.float32)
    cotangent = out_grad[0].astype(jnp.float32)
    order = deal_order[0]
    lengths = seq_lengths[0]
    nseg = lengths.shape[0]
    group_rows = order.shape[0]
    valid_rows = group_rows * 5 // 8
    longest = valid_rows * 4 // 5
    blk = min(512, group_rows)
    keys = min(group_rows, longest + blk)
    nblocks = group_rows // blk
    scale = HEAD_DIM ** (-0.5)
    local_pos = lax.dynamic_slice_in_dim(order, lax.axis_index("seq") * rows, rows)
    local_seg, local_start = segment_of(local_pos, lengths)
    rel = (local_pos - local_start).astype(jnp.float32)
    valid = (local_pos < valid_rows).astype(jnp.float32)[:, None]
    normed1, rstd1 = normalize(stream)
    inverse = (
        jnp.zeros((group_rows,), jnp.int32).at[order].set(jnp.arange(group_rows, dtype=jnp.int32))
    )
    seg_p, start_p = segment_of(jnp.arange(group_rows, dtype=jnp.int32), lengths)

    def to_pack(values):
        heads_here = values.shape[1] // HEAD_DIM
        return values[inverse].reshape(group_rows, heads_here, HEAD_DIM)

    def window(index, packed):
        query_p, key_p, value_p = packed
        first = index * blk
        key_first = jnp.clip(jnp.minimum(start_p[first], group_rows - keys), 0, group_rows - keys)
        qpos = first + jnp.arange(blk, dtype=jnp.int32)
        kpos = key_first + jnp.arange(keys, dtype=jnp.int32)
        qseg = lax.dynamic_slice_in_dim(seg_p, first, blk)
        kseg = lax.dynamic_slice_in_dim(seg_p, key_first, keys)
        allowed = (qseg[:, None] == kseg[None, :]) & (qseg[:, None] < nseg) & (
            kpos[None, :] <= qpos[:, None]
        ) | (kpos[None, :] == qpos[:, None])
        qblock = lax.dynamic_slice_in_dim(query_p, first, blk)
        kblock = lax.dynamic_slice_in_dim(key_p, key_first, keys)
        vblock = lax.dynamic_slice_in_dim(value_p, key_first, keys)
        scores = (
            jnp.einsum("qhd,khd->hqk", qblock, kblock, preferred_element_type=jnp.float32) * scale
        )
        scores = jnp.where(allowed[None], scores, -1e30)
        return (first, key_first, qblock, kblock, vblock, scores)

    def fetch_full(gain, shift, first_w, middle_w, last_w):
        return (
            lax.all_gather(gain, ("seq", "fsdp"), axis=0, tiled=True),
            lax.all_gather(shift, ("seq", "fsdp"), axis=0, tiled=True),
            lax.all_gather(first_w, ("seq", "fsdp"), axis=0, tiled=True),
            lax.all_gather(middle_w, ("seq", "fsdp"), axis=0, tiled=True),
            lax.all_gather(last_w, ("seq", "fsdp"), axis=0, tiled=True),
        )

    def reduce_full(gain, shift, first_w, middle_w, last_w):
        return (
            lax.psum_scatter(gain, ("seq", "fsdp"), scatter_dimension=0, tiled=True),
            lax.psum_scatter(shift, ("seq", "fsdp"), scatter_dimension=0, tiled=True),
            lax.psum_scatter(first_w, ("seq", "fsdp"), scatter_dimension=0, tiled=True),
            lax.psum_scatter(middle_w, ("seq", "fsdp"), scatter_dimension=0, tiled=True),
            lax.psum_scatter(last_w, ("seq", "fsdp"), scatter_dimension=0, tiled=True),
        )

    gain1, shift1, qkv_w, qkv_b, out_w = fetch_full(
        ln1_gain, ln1_bias, qkv_weight, qkv_bias.T, out_weight
    )
    qkv_shift = qkv_b.T.reshape(-1).astype(jnp.float32)
    first_in = (normed1 * gain1.astype(jnp.float32) + shift1.astype(jnp.float32)).astype(
        jnp.bfloat16
    )
    qkv = jnp.dot(first_in, qkv_w, preferred_element_type=jnp.float32) + qkv_shift
    query = rotate(qkv[:, :width], rel, 1.0).astype(jnp.bfloat16)
    keyset = rotate(qkv[:, width : 2 * width], rel, 1.0).astype(jnp.bfloat16)
    valueset = qkv[:, 2 * width :].astype(jnp.bfloat16)
    query, keyset, valueset = (query, keyset, valueset)
    query_h = lax.all_to_all(query, "seq", split_axis=1, concat_axis=0, tiled=True)
    key_h = lax.all_to_all(keyset, "seq", split_axis=1, concat_axis=0, tiled=True)
    value_h = lax.all_to_all(valueset, "seq", split_axis=1, concat_axis=0, tiled=True)
    packed = (to_pack(query_h), to_pack(key_h), to_pack(value_h))

    def attend_block(index):
        first, key_first, qblock, kblock, vblock, scores = window(index, packed)
        top = jnp.max(scores, -1, keepdims=True)
        expo = jnp.exp(scores - top)
        total = jnp.sum(expo, -1, keepdims=True)
        probs = (expo / total).astype(jnp.bfloat16)
        mixed = jnp.einsum("hqk,khd->qhd", probs, vblock, preferred_element_type=jnp.float32)
        return (mixed, (top + jnp.log(total))[..., 0])

    mixed_all, lse_all = lax.map(attend_block, jnp.arange(nblocks, dtype=jnp.int32))
    mixed_pack = mixed_all.reshape(group_rows, -1)
    heads_out = lax.all_to_all(
        mixed_pack[order].astype(jnp.bfloat16), "seq", split_axis=0, concat_axis=1, tiled=True
    )
    heads_out, packed, lse_all = (heads_out, packed, lse_all)
    attn = jnp.dot(heads_out, out_w, preferred_element_type=jnp.float32)
    resid = stream + attn
    gain2, shift2, gate_w, up_w, down_w = fetch_full(
        ln2_gain, ln2_bias, gate_weight, up_weight, down_weight
    )
    normed2, rstd2 = normalize(resid)
    second_in = (normed2 * gain2.astype(jnp.float32) + shift2.astype(jnp.float32)).astype(
        jnp.bfloat16
    )
    gate = jnp.dot(second_in, gate_w, preferred_element_type=jnp.float32)
    upper = jnp.dot(second_in, up_w, preferred_element_type=jnp.float32)
    hidden, sigma = mlp_forward(gate, upper)
    mlp = jnp.dot(hidden, down_w, preferred_element_type=jnp.float32)
    result = resid + mlp
    sums = lax.psum(
        (
            jnp.sum(valid * result * result),
            jnp.sum(valid * attn * attn),
            jnp.sum(valid * mlp * mlp),
        ),
        ("seq", "fsdp"),
    )
    count = valid_rows * lax.axis_size("fsdp") * width
    rms = jnp.sqrt(jnp.stack(sums) / count)
    gain2, shift2, gate_w, up_w, down_w = fetch_full(
        ln2_gain, ln2_bias, gate_weight, up_weight, down_weight
    )
    mlp_grad = cotangent.astype(jnp.bfloat16)
    down_grad = outer(hidden, mlp_grad)
    hidden_grad = times_transposed(mlp_grad, down_w)
    gate_act, up_act = mlp_backward(hidden_grad, gate, upper, sigma)
    gate_grad = outer(second_in, gate_act)
    up_grad = outer(second_in, up_act)
    second_grad = times_transposed(gate_act, gate_w) + times_transposed(up_act, up_w)
    resid_part, gain2_grad, shift2_grad = norm_back(
        second_grad, normed2, rstd2, gain2.astype(jnp.float32)
    )
    resid_grad = cotangent + resid_part
    mlp_shards = reduce_full(gain2_grad, shift2_grad, gate_grad, up_grad, down_grad)
    gain1, shift1, qkv_w, qkv_b, out_w = fetch_full(
        ln1_gain, ln1_bias, qkv_weight, qkv_bias.T, out_weight
    )
    attn_grad = resid_grad.astype(jnp.bfloat16)
    out_grad_w = outer(heads_out, attn_grad)
    mixed_grad = times_transposed(attn_grad, out_w).astype(jnp.bfloat16)
    mixed_grad_p = to_pack(
        lax.all_to_all(mixed_grad, "seq", split_axis=1, concat_axis=0, tiled=True)
    )

    def back_block(index, carry):
        query_acc, key_acc, value_acc = carry
        first, key_first, qblock, kblock, vblock, scores = window(index, packed)
        probs = jnp.exp(scores - lse_all[index][:, :, None])
        dblock = lax.dynamic_slice_in_dim(mixed_grad_p, first, blk)
        value_part = jnp.einsum(
            "hqk,qhd->khd", probs.astype(jnp.bfloat16), dblock, preferred_element_type=jnp.float32
        )
        prob_grad = jnp.einsum("qhd,khd->hqk", dblock, vblock, preferred_element_type=jnp.float32)
        inner = jnp.sum(probs * prob_grad, -1, keepdims=True)
        score_grad = (probs * (prob_grad - inner)).astype(jnp.bfloat16)
        query_part = (
            jnp.einsum("hqk,khd->qhd", score_grad, kblock, preferred_element_type=jnp.float32)
            * scale
        )
        key_part = (
            jnp.einsum("hqk,qhd->khd", score_grad, qblock, preferred_element_type=jnp.float32)
            * scale
        )
        query_acc = lax.dynamic_update_slice_in_dim(query_acc, query_part, first, 0)
        key_old = lax.dynamic_slice_in_dim(key_acc, key_first, keys)
        key_acc = lax.dynamic_update_slice_in_dim(key_acc, key_old + key_part, key_first, 0)
        value_old = lax.dynamic_slice_in_dim(value_acc, key_first, keys)
        value_acc = lax.dynamic_update_slice_in_dim(value_acc, value_old + value_part, key_first, 0)
        return (query_acc, key_acc, value_acc)

    zeros = jnp.zeros(packed[0].shape, jnp.float32)
    query_acc, key_acc, value_acc = lax.fori_loop(0, nblocks, back_block, (zeros, zeros, zeros))

    def to_dealt(values):
        return values.reshape(group_rows, -1)[order].astype(jnp.bfloat16)

    query_g = lax.all_to_all(to_dealt(query_acc), "seq", split_axis=0, concat_axis=1, tiled=True)
    key_g = lax.all_to_all(to_dealt(key_acc), "seq", split_axis=0, concat_axis=1, tiled=True)
    value_g = lax.all_to_all(to_dealt(value_acc), "seq", split_axis=0, concat_axis=1, tiled=True)
    qkv_act = jnp.concatenate(
        [
            rotate(query_g.astype(jnp.float32), rel, -1.0),
            rotate(key_g.astype(jnp.float32), rel, -1.0),
            value_g.astype(jnp.float32),
        ],
        1,
    ).astype(jnp.bfloat16)
    qkv_bias_grad = jnp.sum(qkv_act.astype(jnp.float32), 0).reshape(3, width).T
    qkv_grad = outer(first_in, qkv_act)
    first_grad = times_transposed(qkv_act, qkv_w)
    input_part, gain1_grad, shift1_grad = norm_back(
        first_grad, normed1, rstd1, gain1.astype(jnp.float32)
    )
    input_grad = resid_grad + input_part
    attn_shards = reduce_full(gain1_grad, shift1_grad, qkv_grad, qkv_bias_grad, out_grad_w)
    return (
        result.astype(jnp.bfloat16)[None],
        input_grad[None],
        attn_shards[0],
        attn_shards[1],
        attn_shards[2],
        attn_shards[3].T,
        attn_shards[4],
        mlp_shards[0],
        mlp_shards[1],
        mlp_shards[2],
        mlp_shards[3],
        mlp_shards[4],
        rms,
    )


def solution(mesh):
    in_specs = (
        P("fsdp", "seq", None),
        P(("seq", "fsdp")),
        P(("seq", "fsdp")),
        P(("seq", "fsdp"), None),
        P(None, ("seq", "fsdp")),
        P(("seq", "fsdp"), None),
        P(("seq", "fsdp")),
        P(("seq", "fsdp")),
        P(("seq", "fsdp"), None),
        P(("seq", "fsdp"), None),
        P(("seq", "fsdp"), None),
        P("fsdp", None),
        P("fsdp", None),
        P("fsdp", "seq", None),
    )
    out_specs = (
        P("fsdp", "seq", None),
        P("fsdp", "seq", None),
        P(("seq", "fsdp")),
        P(("seq", "fsdp")),
        P(("seq", "fsdp"), None),
        P(None, ("seq", "fsdp")),
        P(("seq", "fsdp"), None),
        P(("seq", "fsdp")),
        P(("seq", "fsdp")),
        P(("seq", "fsdp"), None),
        P(("seq", "fsdp"), None),
        P(("seq", "fsdp"), None),
        P(),
    )
    return jax.shard_map(body, mesh=mesh, in_specs=in_specs, out_specs=out_specs, check_vma=False)
```

profile of v0, /device:TPU:1, one launch (start us, length us, event | category | flops | bytes accessed | tf_op | source)
XLA Modules:
  0.0 3154.0 jit_solution(16658378083250577882)
XLA Ops:
  11.4 43.8 %all-gather = bf16[32,64,3]{1,2,0:T(4,128)(2,1)S(1)} all-gather(bf16[1,64,3]{1,2,0:T(4,128)(2,1)} %bitcast.252), channel_id=1, replica_groups=mesh['seq'=8,'fsdp'=4] {'seq','fsdp'}, dimensions={0}, use_global_device_ids=true | all-gather | bytes 12672 | tf_op jit(solution)/shard_map/all_gather | solution.py:153
  58.7 37.6 %all-reduce.9 = (bf16[2048]{0:T(1024)(128)(2,1)S(1)}, bf16[2048]{0:T(1024)(128)(2,1)S(1)}, bf16[2048]{0:T(1024)(128)(2,1)S(1)}, bf16[2048]{0:T(1024)(128)(2,1)S(1)}) all-reduce(bf16[2048]{0:T(1024)(128)(2,1)S(1)} %dynamic-update-slice.1, bf16[2048]{0:T(1024)(128)(2,1)S(1)} %dynamic-update-slice, ...), channel_id=1, replica_groups=mesh['seq'=8,'fsdp'=4] {'seq','fsdp'}, use_global_device_ids=true, to_apply=%add.1 | all-reduce | flops 8192 | bytes 32768
  100.1 69.8 %all-gather.7.cloned.1.call-done = bf16[2048,6144]{1,0:T(8,128)(2,1)} async-done(((bf16[64,6144]{1,0:T(8,128)(2,1)}), bf16[2048,6144]{1,0:T(8,128)(2,1)}) %all-gather.7.cloned.1.call-update) | async-done | bytes 25165840 | tf_op jit(solution)/shard_map/all_gather | solution.py:152
  169.9 10.1 convolution_add_fusion
  187.0 20.9 all_to_all.116
  216.9 11.1 all-to-all-done.1
  227.9 13.6 all-to-all-start.2
  266.7 22.6 while.30
  302.5 27.9 all-to-all-done.3
  337.5 81.7 %all-gather.11.cloned.1.call-done = bf16[2048,5632]{1,0:T(8,128)(2,1)} async-done(((bf16[64,5632]{1,0:T(8,128)(2,1)}), bf16[2048,5632]{1,0:T(8,128)(2,1)}) %all-gather.11.cloned.1.call-update) | async-done | bytes 23068688 | tf_op jit(solution)/shard_map/all_gather | solution.py:152
  419.2 12.5 fusion.76
  431.7 133.0 %all-gather.13.cloned.1.call-done = bf16[2048,5632]{1,0:T(8,128)(2,1)} async-done(((bf16[64,5632]{1,0:T(8,128)(2,1)}), bf16[2048,5632]{1,0:T(8,128)(2,1)}) %all-gather.13.cloned.1.call-update) | async-done | bytes 23068688 | tf_op jit(solution)/shard_map/all_gather | solution.py:153
  564.7 12.3 fusion.77
  577.0 133.2 %all-gather.15.cloned.1.call-done = bf16[5632,2048]{1,0:T(8,128)(2,1)} async-done(((bf16[176,2048]{1,0:T(8,128)(2,1)}), bf16[5632,2048]{1,0:T(8,128)(2,1)}) %all-gather.15.cloned.1.call-update) | async-done | bytes 23068688 | tf_op jit(solution)/shard_map/all_gather | solution.py:154
  710.2 15.6 multiply_convert_fusion.1
  725.8 13.4 fusion.78
  739.2 12.2 convolution_add_fusion.1
  751.5 13.5 fusion.53
  773.1 13.7 all-to-all-done.4
  794.7 44.1 %while.31 = (s32[]{:T(128)}, bf16[1024,4,64]{0,2,1:T(8,128)(2,1)}, f32[1024,4,64]{0,2,1:T(8,128)S(1)}, f32[1024,4,64]{0,2,1:T(8,128)}, s32[1024]{0:T(1024)S(1)},...) while((s32[]{:T(128)}, bf16[1024,4,64]{0,2,1:T(8,128)(2,1)}, ...), condition=%wide.region_18.19_spmd.clone, body=%wide.region_16.18_spmd.clone.sunk | while | flops 1378222080 | bytes 164707824 | solution.py:274
  886.1 12.8 all-to-all-done.7
  910.1 20.8 fusion.69
  932.5 18.0 fusion.79
  951.9 18.0 fusion.80
  971.3 18.0 fusion.56
  990.7 20.7 fusion.51
  1011.4 44.7 %all-reduce.8 = (f32[2048]{0:T(1024)S(1)}, f32[2048]{0:T(1024)S(1)}, f32[2048]{0:T(1024)S(1)}, f32[2048]{0:T(1024)S(1)}, f32[1]{0:T(128)}, /*index=5*/f32[1]{0:T(128)}, f32[1]{0:T(128)}) all-reduce(f32[2048]{0:T(1024)S(1)} %get-tuple-element.310, ...), channel_id=2, replica_groups=mesh['seq'=8,'fsdp'=4] {'seq','fsdp'}, use_global_device_ids=true, to_apply=%region_22.23.clone | all-reduce | flops 8195 | bytes 65560
  1065.1 153.7 %reduce-scatter.11.cloned.1.call-done = f32[64,2048]{1,0:T(8,128)} async-done(((f32[2048,2048]{1,0:T(8,128)}), f32[64,2048]{1,0:T(8,128)}) %reduce-scatter.11.cloned.1.call-update) | async-done | bytes 524304 | tf_op jit(solution)/shard_map/reduce_scatter | solution.py:163
  1218.8 441.8 %reduce-scatter.9.cloned.1.call-done = f32[64,6144]{1,0:T(8,128)} async-done(((f32[2048,6144]{1,0:T(8,128)}), f32[64,6144]{1,0:T(8,128)}) %reduce-scatter.9.cloned.1.call-update) | async-done | bytes 1572880 | tf_op jit(solution)/shard_map/reduce_scatter | solution.py:161
  1660.6 494.7 %reduce-scatter.13.cloned.1.call-done = f32[64,5632]{1,0:T(8,128)} async-done(((f32[2048,5632]{1,0:T(8,128)}), f32[64,5632]{1,0:T(8,128)}) %reduce-scatter.13.cloned.1.call-update) | async-done | bytes 1441808 | tf_op jit(solution)/shard_map/reduce_scatter | solution.py:161
  2155.3 495.9 %reduce-scatter.15.cloned.1.call-done = f32[64,5632]{1,0:T(8,128)} async-done(((f32[2048,5632]{1,0:T(8,128)}), f32[64,5632]{1,0:T(8,128)}) %reduce-scatter.15.cloned.1.call-update) | async-done | bytes 1441808 | tf_op jit(solution)/shard_map/reduce_scatter | solution.py:162
  2651.2 496.0 %reduce-scatter.17.cloned.1.call-done = f32[176,2048]{1,0:T(8,128)} async-done(((f32[5632,2048]{1,0:T(8,128)}), f32[176,2048]{1,0:T(8,128)}) %reduce-scatter.17.cloned.1.call-update) | async-done | bytes 1441808 | tf_op jit(solution)/shard_map/reduce_scatter | solution.py:163
  (306 shorter events, 223.9 us)
Async XLA Ops:
  7.2 91.9 %copy-start.3 = (bf16[1,128,2048]{2,1,0:T(8,128)(2,1)S(1)}, bf16[1,128,2048]{2,1,0:T(8,128)(2,1)}, u32[]{:S(2)}) copy-start(bf16[1,128,2048]{2,1,0:T(8,128)(2,1)} %param.18) | copy-start | bytes 1572868
  7.2 162.7 %all-gather.7.cloned.1.call-start = ((), (), s32[]{:S(2)}) async-start(), calls=%async_computation.14 | async-start | bytes 25952256 | tf_op jit(solution)/shard_map/all_gather | solution.py:152
  7.9 294.5 %all-gather.9.cloned.1.call-start = ((), (), s32[]{:S(2)}) async-start(), calls=%async_computation.15 | async-start | bytes 8650752 | tf_op jit(solution)/shard_map/all_gather | solution.py:154
  8.7 410.5 %all-gather.11.cloned.1.call-start = ((), (), s32[]{:S(2)}) async-start(), calls=%async_computation.16 | async-start | bytes 23789568 | tf_op jit(solution)/shard_map/all_gather | solution.py:152
  9.4 555.3 %all-gather.13.cloned.1.call-start = ((), (), s32[]{:S(2)}) async-start(), calls=%async_computation.17 | async-start | bytes 23789568 | tf_op jit(solution)/shard_map/all_gather | solution.py:153
  10.0 700.2 %all-gather.15.cloned.1.call-start = ((), (), s32[]{:S(2)}) async-start(), calls=%async_computation.18 | async-start | bytes 23789568 | tf_op jit(solution)/shard_map/all_gather | solution.py:154
  96.4 83.7 %copy-start.33 = (f32[2048]{0:T(1024)}, f32[2048]{0:T(1024)S(1)}, u32[]{:S(2)}) copy-start(f32[2048]{0:T(1024)S(1)} %convert_element_type.172) | copy-start | bytes 24580
  96.4 83.7 %copy-start.29 = (f32[2048]{0:T(1024)}, f32[2048]{0:T(1024)S(1)}, u32[]{:S(2)}) copy-start(f32[2048]{0:T(1024)S(1)} %convert_element_type.171) | copy-start | bytes 24580
  99.1 81.0 %copy-start.41 = (f32[128]{0:T(128)}, f32[128]{0:T(128)S(1)}, u32[]{:S(2)}) copy-start(f32[128]{0:T(128)S(1)} %broadcast_multiply_fusion.6) | copy-start | bytes 1540
  99.4 80.7 %copy-start.45 = (f32[128]{0:T(128)}, f32[128]{0:T(128)S(1)}, u32[]{:S(2)}) copy-start(f32[128]{0:T(128)S(1)} %add_rsqrt_fusion.1) | copy-start | bytes 1540
  100.1 84.9 %copy-start.39 = (f32[128,8]{0,1:T(8,128)}, f32[128,8]{0,1:T(8,128)S(1)}, u32[]{:S(2)}) copy-start(f32[128,8]{0,1:T(8,128)S(1)} %get-tuple-element.405) | copy-start | bytes 12292
  185.0 56.6 %copy-start.48 = (s32[1,1024]{1,0:T(1,128)S(1)}, s32[1,1024]{1,0:T(1,128)}, u32[]{:S(2)}) copy-start(s32[1,1024]{1,0:T(1,128)} %param.30) | copy-start | bytes 12292
  207.8 20.1 all-to-all-start.1
  227.9 34.5 %all-to-all-start.2 = ((bf16[128,8,256]{2,0,1:T(8,128)(2,1)}), bf16[128,8,256]{2,0,1:T(8,128)(2,1)S(1)}, u32[]{:S(2)}, u32[]{:S(2)}) async-start(bf16[128,8,256]{2,0,1:T(8,128)(2,1)} %bitcast.173), calls=%async_computation.2 | async-start | bytes 1048576 | tf_op jit(solution)/shard_map/all_to_all | solution.py:180
  247.0 46.7 %copy-start.35 = (s32[1024]{0:T(1024)}, s32[1024]{0:T(1024)S(1)}, u32[]{:S(2)}) copy-start(s32[1024]{0:T(1024)S(1)} %broadcast_clamp_fusion) | copy-start | bytes 12292
  298.6 31.7 %all-to-all-start.3 = ((bf16[8,128,256]{1,2,0:T(8,128)(2,1)}), bf16[8,128,256]{1,2,0:T(8,128)(2,1)S(1)}, u32[]{:S(2)}, u32[]{:S(2)}) async-start(bf16[8,128,256]{1,2,0:T(8,128)(2,1)} %copy.115), calls=%async_computation.3 | async-start | bytes 1048576 | tf_op jit(solution)/shard_map/all_to_all | solution.py:194
  337.5 227.2 %copy-start.7 = (bf16[128,2048]{1,0:T(8,128)(2,1)}, bf16[128,2048]{1,0:T(8,128)(2,1)S(1)}, u32[]{:S(2)}) copy-start(bf16[128,2048]{1,0:T(8,128)(2,1)S(1)} %add_convert_fusion) | copy-start | bytes 1572868
  765.6 21.1 copy-start.38
  769.4 17.4 all-to-all-start.4
  794.7 44.3 %copy-start.36 = (s32[1024]{0:T(1024)S(1)}, s32[1024]{0:T(1024)}, u32[]{:S(2)}) copy-start(s32[1024]{0:T(1024)} %copy-done.35) | copy-start | bytes 12292
  843.9 18.0 all-to-all-start.6
  862.0 18.7 all-to-all-start.5
  880.6 18.3 all-to-all-start.7
  885.5 178.2 %reduce-scatter.19.cloned.1.call-start = ((), (), s32[]{:S(2)}) async-start(), calls=%async_computation.24 | async-start | bytes 1081344
  886.0 23.1 copy-start.20
  886.1 23.1 copy-start.22
  900.9 317.9 %reduce-scatter.11.cloned.1.call-start = ((), (), s32[]{:S(2)}) async-start(), calls=%async_computation.20 | async-start | bytes 17301504 | tf_op jit(solution)/shard_map/reduce_scatter | solution.py:163
  909.1 751.5 %reduce-scatter.9.cloned.1.call-start = ((), (), s32[]{:S(2)}) async-start(), calls=%async_computation.19 | async-start | bytes 51904512 | tf_op jit(solution)/shard_map/reduce_scatter | solution.py:161
  931.0 1224.3 %reduce-scatter.13.cloned.1.call-start = ((), (), s32[]{:S(2)}) async-start(), calls=%async_computation.21 | async-start | bytes 47579136 | tf_op jit(solution)/shard_map/reduce_scatter | solution.py:161
  950.5 1700.7 %reduce-scatter.15.cloned.1.call-start = ((), (), s32[]{:S(2)}) async-start(), calls=%async_computation.22 | async-start | bytes 47579136 | tf_op jit(solution)/shard_map/reduce_scatter | solution.py:162
  969.9 2177.4 %reduce-scatter.17.cloned.1.call-start = ((), (), s32[]{:S(2)}) async-start(), calls=%async_computation.23 | async-start | bytes 47579136 | tf_op jit(solution)/shard_map/reduce_scatter | solution.py:163
  990.7 20.7 copy-start.44
  (48 other events, 260.4 us)
Sparse Core Ops, SparseCore 0:
  10.9 158.9 all-gather.6
  172.8 90.7 all-gather.8
  266.4 152.7 all-gather.10
  421.9 142.7 all-gather.12
  567.4 142.7 all-gather.14
  901.1 129.6 reduce-scatter.18
  1033.7 185.0 reduce-scatter.10
  1226.9 433.6 reduce-scatter.8
  1663.6 491.6 reduce-scatter.12
  2158.1 493.0 reduce-scatter.14
  2654.2 493.0 reduce-scatter.16
where the time goes:
time: 3160 us; the launch traced here: 3150 us
  waiting for transfers between devices  2590 us (82%)
  matrix products  238 us (8%)
  blocking collectives  147 us (5%)
  local copies, waits for them, and re-layouts  88.9 us (3%)
  starting transfers between devices  43.1 us (1%)
    reduce_scatter x2, waiting for transfers between devices, reduce_full(): lax.psum_scatter(first_w, ('seq', 'fsdp'), scatter_dimension=0, tiled=True)  936 us
    reduce_scatter x2, waiting for transfers between devices, reduce_full(): lax.psum_scatter(last_w, ('seq', 'fsdp'), scatter_dimension=0, tiled=True)  650 us
    reduce_scatter x1, waiting for transfers between devices, reduce_full(): lax.psum_scatter(middle_w, ('seq', 'fsdp'), scatter_dimension=0, tiled=True)  496 us
    all_gather x2, waiting for transfers between devices, fetch_full(): lax.all_gather(first_w, ('seq', 'fsdp'), axis=0, tiled=True)  151 us
    all_gather x2, waiting for transfers between devices, fetch_full(): lax.all_gather(last_w, ('seq', 'fsdp'), axis=0, tiled=True)  133 us
    all_gather x1, waiting for transfers between devices, fetch_full(): lax.all_gather(middle_w, ('seq', 'fsdp'), axis=0, tiled=True)  133 us
    dot_general x5, matrix products, outer(): lax.dot_general(left, right, (((0,), (0,)), ((), ())), preferred_element_...  82.9 us
    unnamed x2, blocking collectives  82.4 us
  transfers between devices with their start and end apart: 18, of which 16 were waited for; matrix products, arithmetic and copies ran while one was open for 7% of the time, Pallas kernels for 0%

commit v1 on v0

--- a/solution.py
+++ b/solution.py
@@ -6,6 +6,18 @@
 HEAD_DIM = 64
 ROT = 16
 EPS = 1e-05
+
+
+def doubled_up(shard, axis, dim):
+    ways, here = (lax.axis_size(axis), lax.axis_index(axis))
+    grown, reach = (shard, 1)
+    while reach < ways:
+        theirs = lax.ppermute(grown, axis, [(d, d ^ reach) for d in range(ways)])
+        mine_first = jnp.concatenate([grown, theirs], axis=dim)
+        theirs_first = jnp.concatenate([theirs, grown], axis=dim)
+        grown = jnp.where(here & reach == 0, mine_first, theirs_first)
+        reach = 2 * reach
+    return grown
 
 
 def normalize(values):
@@ -150,7 +162,7 @@
             lax.all_gather(gain, ("seq", "fsdp"), axis=0, tiled=True),
             lax.all_gather(shift, ("seq", "fsdp"), axis=0, tiled=True),
             lax.all_gather(first_w, ("seq", "fsdp"), axis=0, tiled=True),
-            lax.all_gather(middle_w, ("seq", "fsdp"), axis=0, tiled=True),
+            doubled_up(middle_w, ("seq", "fsdp"), 0),
             lax.all_gather(last_w, ("seq", "fsdp"), axis=0, tiled=True),
         )
 

time: 3160 us -> 3640 us (1.15)
  waiting for transfers between devices: 2590 us -> 3040 us
    all_to_all x1, waiting for transfers between devices: 27.9 us -> 545 us  [body(): lax.all_to_all(mixed_pack[order].astype(jnp.bfloat16), 'seq', split_axis=...]
    ppermute x0 -> x10, waiting for transfers between devices: none -> 359 us  [doubled_up(): theirs = lax.ppermute(grown, axis, [(d, d ^ reach) for d in range(ways)])]
    all_gather x2, waiting for transfers between devices: 151 us -> 0.04 us  [fetch_full(): lax.all_gather(first_w, ('seq', 'fsdp'), axis=0, tiled=True)]
    all_gather x2, waiting for transfers between devices: 133 us -> 0.02 us  [fetch_full(): lax.all_gather(last_w, ('seq', 'fsdp'), axis=0, tiled=True)]
    all_gather x1 -> x0, waiting for transfers between devices: 133 us -> none  [fetch_full(): lax.all_gather(middle_w, ('seq', 'fsdp'), axis=0, tiled=True)]
    all_gather x1 -> x0, blocking collectives: 43.8 us -> none  [fetch_full(): lax.all_gather(middle_w, ('seq', 'fsdp'), axis=0, tiled=True)]
  transfers between devices with their start and end apart: 18 -> 27, of which waited for: 16 -> 16; matrix products, arithmetic and copies ran while one was open for 7% -> 7% of each run, Pallas kernels for 0% -> 0%
where the time goes in v1:
time: 3640 us; the launch traced here: 3630 us
  waiting for transfers between devices  3040 us (84%)
  matrix products  252 us (7%)
  blocking collectives  114 us (3%)
  local copies, waits for them, and re-layouts  89.3 us (2%)
  starting transfers between devices  57.9 us (2%)
  other arithmetic  52.8 us (1%)
    reduce_scatter x2, waiting for transfers between devices, reduce_full(): lax.psum_scatter(first_w, ('seq', 'fsdp'), scatter_dimension=0, tiled=True)  937 us
    reduce_scatter x2, waiting for transfers between devices, reduce_full(): lax.psum_scatter(last_w, ('seq', 'fsdp'), scatter_dimension=0, tiled=True)  650 us
    all_to_all x1, waiting for transfers between devices, body(): lax.all_to_all(mixed_pack[order].astype(jnp.bfloat16), 'seq', split_axis=...  545 us
    reduce_scatter x1, waiting for transfers between devices, reduce_full(): lax.psum_scatter(middle_w, ('seq', 'fsdp'), scatter_dimension=0, tiled=True)  496 us
    ppermute x10, waiting for transfers between devices, doubled_up(): theirs = lax.ppermute(grown, axis, [(d, d ^ reach) for d in range(ways)])  359 us
    unnamed x2, blocking collectives  92.9 us
    dot_general x5, matrix products, outer(): lax.dot_general(left, right, (((0,), (0,)), ((), ())), preferred_element_...  83 us
  transfers between devices with their start and end apart: 27, of which 16 were waited for; matrix products, arithmetic and copies ran while one was open for 7% of the time, Pallas kernels for 0%

profile of v1, /device:TPU:1, one launch (start us, length us, event | category | flops | bytes accessed | tf_op | source)
XLA Modules:
  0.0 3628.4 jit_solution(10556095188077278237)
XLA Ops:
  16.5 38.0 %collective-permute-done.6 = bf16[128,5632]{1,0:T(8,128)(2,1)S(1)} collective-permute-done((bf16[128,5632]{1,0:T(8,128)(2,1)S(1)}, bf16[128,5632]{1,0:T(8,128)(2,1)S(1)}, u32[]{:S(2)}, u32[]{:S(2)}) %collective-permute-start.6) | collective-permute-done | bytes 1441824 | tf_op jit(solution)/shard_map/ppermute | solution.py:15
  66.4 83.9 %collective-permute-done.7 = bf16[256,5632]{1,0:T(8,128)(2,1)} collective-permute-done((bf16[256,5632]{1,0:T(8,128)(2,1)}, bf16[256,5632]{1,0:T(8,128)(2,1)}, u32[]{:S(2)}, u32[]{:S(2)}) %collective-permute-start.7) | collective-permute-done | bytes 2883616 | tf_op jit(solution)/shard_map/ppermute | solution.py:15
  160.3 233.4 %collective-permute-done.3 = bf16[512,3]{0,1:T(4,128)(2,1)S(1)} collective-permute-done((bf16[512,3]{0,1:T(4,128)(2,1)S(1)}, bf16[512,3]{0,1:T(4,128)(2,1)S(1)}, u32[]{:S(2)}, u32[]{:S(2)}) %collective-permute-start.3) | collective-permute-done | bytes 3104 | tf_op jit(solution)/shard_map/ppermute | solution.py:15
  400.9 48.6 %all-reduce.9 = (bf16[2048]{0:T(1024)(128)(2,1)S(1)}, bf16[2048]{0:T(1024)(128)(2,1)S(1)}, bf16[2048]{0:T(1024)(128)(2,1)S(1)}, bf16[2048]{0:T(1024)(128)(2,1)S(1)}) all-reduce(bf16[2048]{0:T(1024)(128)(2,1)S(1)} %dynamic-update-slice.1, bf16[2048]{0:T(1024)(128)(2,1)S(1)} %dynamic-update-slice, ...), channel_id=1, replica_groups=mesh['seq'=8,'fsdp'=4] {'seq','fsdp'}, use_global_device_ids=true, to_apply=%add.1 | all-reduce | flops 8192 | bytes 32768
  450.1 10.4 convolution_add_fusion
  467.2 20.9 all_to_all.116
  488.1 11.3 all-to-all-start.1
  506.1 12.6 all-to-all-done.1
  522.5 16.4 maximum_select_fusion.1
  554.2 22.6 while.30
  592.2 13.9 fusion.61
  606.1 544.9 %all-to-all-done.3 = bf16[8,128,256]{1,2,0:T(8,128)(2,1)S(1)} async-done(((bf16[8,128,256]{1,2,0:T(8,128)(2,1)}), bf16[8,128,256]{1,2,0:T(8,128)(2,1)S(1)}, u32[]{:S(2)}, u32[]{:S(2)}) %all-to-all-start.3) | async-done | bytes 524320 | tf_op jit(solution)/shard_map/all_to_all | solution.py:206
  1158.2 12.5 fusion.81
  1170.7 19.2 multiply_convert_fusion.1
  1189.9 13.9 fusion.82
  1203.8 17.8 fusion.38
  1221.7 12.8 fusion.56
  1247.6 13.4 all-to-all-done.4
  1268.9 44.1 %while.31 = (s32[]{:T(128)}, bf16[1024,4,64]{0,2,1:T(8,128)(2,1)}, f32[1024,4,64]{0,2,1:T(8,128)S(1)}, f32[1024,4,64]{0,2,1:T(8,128)}, s32[1024]{0:T(1024)S(1)},...) while((s32[]{:T(128)}, bf16[1024,4,64]{0,2,1:T(8,128)(2,1)}, ...), condition=%wide.region_18.19_spmd.clone, body=%wide.region_16.18_spmd.clone.sunk | while | flops 1378222080 | bytes 164707824 | solution.py:286
  1328.2 8.3 all-to-all-done.6
  1360.4 12.8 all-to-all-done.7
  1384.4 20.8 fusion.74
  1406.7 18.0 fusion.83
  1426.1 18.0 fusion.84
  1445.6 18.1 fusion.59
  1465.0 20.6 fusion.54
  1485.6 44.3 %all-reduce.8 = (f32[2048]{0:T(1024)S(1)}, f32[2048]{0:T(1024)S(1)}, f32[2048]{0:T(1024)S(1)}, f32[2048]{0:T(1024)S(1)}, f32[1]{0:T(128)}, /*index=5*/f32[1]{0:T(128)}, f32[1]{0:T(128)}) all-reduce(f32[2048]{0:T(1024)S(1)} %get-tuple-element.310, ...), channel_id=2, replica_groups=mesh['seq'=8,'fsdp'=4] {'seq','fsdp'}, use_global_device_ids=true, to_apply=%region_22.23.clone | all-reduce | flops 8195 | bytes 65560
  1538.8 153.8 %reduce-scatter.11.cloned.1.call-done = f32[64,2048]{1,0:T(8,128)} async-done(((f32[2048,2048]{1,0:T(8,128)}), f32[64,2048]{1,0:T(8,128)}) %reduce-scatter.11.cloned.1.call-update) | async-done | bytes 524304 | tf_op jit(solution)/shard_map/reduce_scatter | solution.py:175
  1692.6 441.9 %reduce-scatter.9.cloned.1.call-done = f32[64,6144]{1,0:T(8,128)} async-done(((f32[2048,6144]{1,0:T(8,128)}), f32[64,6144]{1,0:T(8,128)}) %reduce-scatter.9.cloned.1.call-update) | async-done | bytes 1572880 | tf_op jit(solution)/shard_map/reduce_scatter | solution.py:173
  2134.5 494.7 %reduce-scatter.13.cloned.1.call-done = f32[64,5632]{1,0:T(8,128)} async-done(((f32[2048,5632]{1,0:T(8,128)}), f32[64,5632]{1,0:T(8,128)}) %reduce-scatter.13.cloned.1.call-update) | async-done | bytes 1441808 | tf_op jit(solution)/shard_map/reduce_scatter | solution.py:173
  2629.2 496.1 %reduce-scatter.15.cloned.1.call-done = f32[64,5632]{1,0:T(8,128)} async-done(((f32[2048,5632]{1,0:T(8,128)}), f32[64,5632]{1,0:T(8,128)}) %reduce-scatter.15.cloned.1.call-update) | async-done | bytes 1441808 | tf_op jit(solution)/shard_map/reduce_scatter | solution.py:174
  3125.3 495.9 %reduce-scatter.17.cloned.1.call-done = f32[176,2048]{1,0:T(8,128)} async-done(((f32[5632,2048]{1,0:T(8,128)}), f32[176,2048]{1,0:T(8,128)}) %reduce-scatter.17.cloned.1.call-update) | async-done | bytes 1441808 | tf_op jit(solution)/shard_map/reduce_scatter | solution.py:175
  (340 shorter events, 241.7 us)
Async XLA Ops:
  7.2 442.4 %all-gather.5.cloned.1.call-start = ((), (), s32[]{:S(2)}) async-start(), calls=%async_computation.14 | async-start | bytes 25952256 | tf_op jit(solution)/shard_map/all_gather | solution.py:164
  8.0 584.3 %all-gather.11.cloned.1.call-start = ((), (), s32[]{:S(2)}) async-start(), calls=%async_computation.17 | async-start | bytes 23789568 | tf_op jit(solution)/shard_map/all_gather | solution.py:166
  8.7 597.4 %all-gather.7.cloned.1.call-start = ((), (), s32[]{:S(2)}) async-start(), calls=%async_computation.15 | async-start | bytes 8650752 | tf_op jit(solution)/shard_map/all_gather | solution.py:166
  9.4 1148.8 %all-gather.9.cloned.1.call-start = ((), (), s32[]{:S(2)}) async-start(), calls=%async_computation.16 | async-start | bytes 23789568 | tf_op jit(solution)/shard_map/all_gather | solution.py:164
  10.0 2.5 collective-permute-start.5
  14.1 40.4 %collective-permute-start.6 = (bf16[128,5632]{1,0:T(8,128)(2,1)S(1)}, bf16[128,5632]{1,0:T(8,128)(2,1)S(1)}, u32[]{:S(2)}, u32[]{:S(2)}) collective-permute-start(bf16[128,5632]{1,0:T(8,128)(2,1)S(1)} %maximum_select_fusion.8), channel_id=1, source_target_pairs={{0,2},{1,3},{2,0},{3,1},{4,6},{5,7},{6,4},{7,5},{8,10},{9,11},{10,... | collective-permute-start | bytes 4325384 | tf_op jit(solution)/shard_map/ppermute | solution.py:15
  56.5 93.9 %collective-permute-start.7 = (bf16[256,5632]{1,0:T(8,128)(2,1)}, bf16[256,5632]{1,0:T(8,128)(2,1)}, u32[]{:S(2)}, u32[]{:S(2)}) collective-permute-start(bf16[256,5632]{1,0:T(8,128)(2,1)} %maximum_select_fusion.5), channel_id=1, source_target_pairs={{0,4},{1,5},{2,6},{3,7},{4,0},{5,1},{6,2},{7,3},{8,12},{9,13},{10,... | collective-permute-start | bytes 8650760 | tf_op jit(solution)/shard_map/ppermute | solution.py:15
  57.6 4.7 collective-permute-start
  62.3 402.9 %copy-start.42 = (f32[128,8]{0,1:T(8,128)}, f32[128,8]{0,1:T(8,128)S(1)}, u32[]{:S(2)}) copy-start(f32[128,8]{0,1:T(8,128)S(1)} %get-tuple-element.405) | copy-start | bytes 12292
  62.4 3.5 collective-permute-start.1
  65.9 334.0 %copy-start.55 = (bf16[64]{0:T(256)(128)(2,1)S(1)}, bf16[64]{0:T(256)(128)(2,1)}, u32[]{:S(2)}) copy-start(bf16[64]{0:T(256)(128)(2,1)} %param.20) | copy-start | bytes 388
  65.9 334.2 %copy-start.56 = (bf16[64]{0:T(256)(128)(2,1)S(1)}, bf16[64]{0:T(256)(128)(2,1)}, u32[]{:S(2)}) copy-start(bf16[64]{0:T(256)(128)(2,1)} %param.19) | copy-start | bytes 388
  65.9 334.5 %copy-start.57 = (bf16[64]{0:T(256)(128)(2,1)S(1)}, bf16[64]{0:T(256)(128)(2,1)}, u32[]{:S(2)}) copy-start(bf16[64]{0:T(256)(128)(2,1)} %param.25) | copy-start | bytes 388
  65.9 334.7 %copy-start.58 = (bf16[64]{0:T(256)(128)(2,1)S(1)}, bf16[64]{0:T(256)(128)(2,1)}, u32[]{:S(2)}) copy-start(bf16[64]{0:T(256)(128)(2,1)} %param.24) | copy-start | bytes 388
  65.9 93.8 %collective-permute-start.2 = (bf16[256,3]{0,1:T(4,128)(2,1)S(1)}, bf16[256,3]{0,1:T(4,128)(2,1)S(1)}, u32[]{:S(2)}, u32[]{:S(2)}) collective-permute-start(bf16[256,3]{0,1:T(4,128)(2,1)S(1)} %maximum_select_fusion.12), channel_id=1, source_target_pairs={{0,4},{1,5},{2,6},{3,7},{4,0},{5,1},{6,2},{7,3},{8,12},{9,13},{10,... | collective-permute-start | bytes 4616 | tf_op jit(solution)/shard_map/ppermute | solution.py:15
  158.5 364.0 %collective-permute-start.8 = (bf16[512,5632]{1,0:T(8,128)(2,1)}, bf16[512,5632]{1,0:T(8,128)(2,1)}, u32[]{:S(2)}, u32[]{:S(2)}) collective-permute-start(bf16[512,5632]{1,0:T(8,128)(2,1)} %maximum_select_fusion.2), channel_id=1, source_target_pairs={{0,8},{1,9},{2,10},{3,11},{4,12},{5,13},{6,14},{7,15},{8,0},{9,1},... | collective-permute-start | bytes 17301512 | tf_op jit(solution)/shard_map/ppermute | solution.py:15
  159.7 233.9 %collective-permute-start.3 = (bf16[512,3]{0,1:T(4,128)(2,1)S(1)}, bf16[512,3]{0,1:T(4,128)(2,1)S(1)}, u32[]{:S(2)}, u32[]{:S(2)}) collective-permute-start(bf16[512,3]{0,1:T(4,128)(2,1)S(1)} %maximum_select_fusion.11), channel_id=1, source_target_pairs={{0,8},{1,9},{2,10},{3,11},{4,12},{5,13},{6,14},{7,15},{8,0},{9,1},... | collective-permute-start | bytes 9224 | tf_op jit(solution)/shard_map/ppermute | solution.py:15
  393.7 55.9 %collective-permute-start.4 = (bf16[1024,3]{0,1:T(4,128)(2,1)S(1)}, bf16[1024,3]{0,1:T(4,128)(2,1)S(1)}, u32[]{:S(2)}, u32[]{:S(2)}) collective-permute-start(bf16[1024,3]{0,1:T(4,128)(2,1)S(1)} %maximum_select_fusion.10), channel_id=1, source_target_pairs={{0,16},{1,17},{2,18},{3,19},{4,20},{5,21},{6,22},{7,23},{8,24},{9,... | collective-permute-start | bytes 18440 | tf_op jit(solution)/shard_map/ppermute | solution.py:15
  488.1 30.6 all-to-all-start.1
  518.7 31.4 all-to-all-start.2
  538.9 631.8 %collective-permute-start.9 = (bf16[1024,5632]{1,0:T(8,128)(2,1)}, bf16[1024,5632]{1,0:T(8,128)(2,1)}, u32[]{:S(2)}, u32[]{:S(2)}) collective-permute-start(bf16[1024,5632]{1,0:T(8,128)(2,1)} %maximum_select_fusion.1), channel_id=1, source_target_pairs={{0,16},{1,17},{2,18},{3,19},{4,20},{5,21},{6,22},{7,23},{8,24},{9,... | collective-permute-start | bytes 34603016 | tf_op jit(solution)/shard_map/ppermute | solution.py:15
  588.3 562.7 %all-to-all-start.3 = ((bf16[8,128,256]{1,2,0:T(8,128)(2,1)}), bf16[8,128,256]{1,2,0:T(8,128)(2,1)S(1)}, u32[]{:S(2)}, u32[]{:S(2)}) async-start(bf16[8,128,256]{1,2,0:T(8,128)(2,1)} %copy.92), calls=%async_computation.3 | async-start | bytes 1048576 | tf_op jit(solution)/shard_map/all_to_all | solution.py:206
  1243.2 17.8 all-to-all-start.4
  1318.1 18.4 all-to-all-start.6
  1336.5 18.4 all-to-all-start.5
  1355.0 18.3 all-to-all-start.7
  1359.8 177.6 %reduce-scatter.19.cloned.1.call-start = ((), (), s32[]{:S(2)}) async-start(), calls=%async_computation.23 | async-start | bytes 1081344
  1375.2 317.4 %reduce-scatter.11.cloned.1.call-start = ((), (), s32[]{:S(2)}) async-start(), calls=%async_computation.19 | async-start | bytes 17301504 | tf_op jit(solution)/shard_map/reduce_scatter | solution.py:175
  1383.4 751.1 %reduce-scatter.9.cloned.1.call-start = ((), (), s32[]{:S(2)}) async-start(), calls=%async_computation.18 | async-start | bytes 51904512 | tf_op jit(solution)/shard_map/reduce_scatter | solution.py:173
  1405.3 1223.9 %reduce-scatter.13.cloned.1.call-start = ((), (), s32[]{:S(2)}) async-start(), calls=%async_computation.20 | async-start | bytes 47579136 | tf_op jit(solution)/shard_map/reduce_scatter | solution.py:173
  1424.8 1700.5 %reduce-scatter.15.cloned.1.call-start = ((), (), s32[]{:S(2)}) async-start(), calls=%async_computation.21 | async-start | bytes 47579136 | tf_op jit(solution)/shard_map/reduce_scatter | solution.py:174
  1444.1 2177.0 %reduce-scatter.17.cloned.1.call-start = ((), (), s32[]{:S(2)}) async-start(), calls=%async_computation.22 | async-start | bytes 47579136 | tf_op jit(solution)/shard_map/reduce_scatter | solution.py:175
  (63 other events, 1120.1 us)
Sparse Core Ops, SparseCore 0:
  10.9 206.1 all-gather.4
  220.0 204.8 all-gather.10
  427.7 91.4 all-gather.6
  521.9 446.6 all-gather.8
  1375.3 129.4 reduce-scatter.18
  1507.6 184.9 reduce-scatter.10
  1700.8 433.6 reduce-scatter.8
  2137.5 491.6 reduce-scatter.12
  2632.2 493.0 reduce-scatter.14
  3128.1 493.0 reduce-scatter.16
